TPU v7x, 32 devices: a whole 2x2x4 slice. The times are simulated.
32 devices in a mesh: pb: 8 (over y, x, core), kv: 4 (over z).
Axes of the slice: x: 2, y: 2, z: 4, core: 2. Of those that a mesh axis runs over, the one named last changes fastest.
Arguments:
- queries: bfloat16 [4096, 1024], P(('pb', 'kv')), may hold values from -6 to 6
- key_rows: bfloat16 [4096, 128], P(('kv', 'pb')), may hold values from -6 to 6
- value_rows: bfloat16 [4096, 128], P(('kv', 'pb')), may hold values from -0.59765625 to 0.59765625
- output: bfloat16 [4096, 1024], P(('pb', 'kv')), may hold values from -1.796875 to 1.796875
- out_grad: bfloat16 [4096, 1024], P(('pb', 'kv')), may hold values from -6 to 6
- log_norm: float32 [8, 4096], P(None, ('pb', 'kv')), as said below
- positions: int32 [4096], replicated, may hold values from 0 to 4095, as said below
Outputs:
- query_grad: float32 [4096, 1024], P(('pb', 'kv'))
- key_grad: float32 [4096, 128], P(('kv', 'pb'))
- value_grad: float32 [4096, 128], P(('kv', 'pb'))
Inputs may be any that keep to these rules, and one draw needn't show every extreme that they name: A permutation of 0 to 4095: row r holds the token at position positions[r]. log_norm[h, r] - log(1 + positions[r]) lies between 0.25 and 0.75.
All inputs are finite; a program needn't handle non-finite values.
Results may differ from a plain program's by a relative error of at most 0.0041.
Values may be sent and summed in bfloat16 or wider, within the bound.
A program may use at most 64 MiB of HBM per device.

v0:
```python
import math

import jax
import jax.numpy as jnp
from jax import lax
from jax.sharding import PartitionSpec as P


def block_grads(query_all, grad_all, norm_all, delta_all, query_pos, key_part, value_part, key_pos):
    query_count = query_all.shape[0]
    head_count = norm_all.shape[0]
    head_width = key_part.shape[1]
    inv_root = 1.0 / math.sqrt(head_width)
    rows_block = min(query_count, 128)
    count_blocks = query_count // rows_block
    query_blocks = query_all.reshape(count_blocks, rows_block, head_count, head_width)
    grad_blocks = grad_all.reshape(count_blocks, rows_block, head_count, head_width)
    norm_blocks = norm_all.T.reshape(count_blocks, rows_block, head_count)
    delta_blocks = delta_all.T.reshape(count_blocks, rows_block, head_count)
    pos_blocks = query_pos.reshape(count_blocks, rows_block)

    def one_block(running, inputs):
        key_sum, value_sum = running
        query_block, grad_block, norm_block, delta_block, pos_block = inputs
        scores = (
            jnp.einsum("tgd,cd->tgc", query_block, key_part, preferred_element_type=jnp.float32)
            * inv_root
        )
        visible = (key_pos[None, :] <= pos_block[:, None])[:, None, :]
        probs_full = jnp.where(visible, jnp.exp(scores - norm_block[:, :, None]), 0.0)
        probs_low = probs_full.astype(jnp.bfloat16)
        value_sum = value_sum + jnp.einsum(
            "tgc,tgd->cd", probs_low, grad_block, preferred_element_type=jnp.float32
        )
        grad_probs = jnp.einsum(
            "tgd,cd->tgc", grad_block, value_part, preferred_element_type=jnp.float32
        )
        grad_scores = (probs_full * (grad_probs - delta_block[:, :, None]) * inv_root).astype(
            jnp.bfloat16
        )
        query_part = jnp.einsum(
            "tgc,cd->tgd", grad_scores, key_part, preferred_element_type=jnp.float32
        )
        key_sum = key_sum + jnp.einsum(
            "tgc,tgd->cd", grad_scores, query_block, preferred_element_type=jnp.float32
        )
        return ((key_sum, value_sum), query_part.reshape(rows_block, head_count * head_width))

    empty_grad = jnp.zeros((key_part.shape[0], head_width), jnp.float32)
    (key_sum, value_sum), query_parts = lax.scan(
        one_block,
        (empty_grad, empty_grad),
        (query_blocks, grad_blocks, norm_blocks, delta_blocks, pos_blocks),
    )
    return (query_parts.reshape(query_count, head_count * head_width), key_sum, value_sum)


def row_terms(grad_rows, saved_rows, head_count, head_width):
    local_rows = grad_rows.shape[0]
    product = grad_rows.astype(jnp.float32) * saved_rows.astype(jnp.float32)
    return jnp.sum(product.reshape(local_rows, head_count, head_width), axis=2).T


def shards(queries, key_rows, value_rows, output, out_grad, log_norm, positions):
    head_count = log_norm.shape[0]
    head_width = key_rows.shape[1]
    query_count = queries.shape[0] * lax.axis_size("kv")
    key_count = key_rows.shape[0] * lax.axis_size("pb")
    query_pos = lax.dynamic_slice_in_dim(positions, lax.axis_index("pb") * query_count, query_count)
    key_pos = lax.dynamic_slice_in_dim(positions, lax.axis_index("kv") * key_count, key_count)
    local_delta = row_terms(out_grad, output, head_count, head_width)
    query_all, grad_all = (
        lax.all_gather(queries, "kv", axis=0, tiled=True),
        lax.all_gather(out_grad, "kv", axis=0, tiled=True),
    )
    norm_all, delta_all = (
        lax.all_gather(log_norm, "kv", axis=1, tiled=True),
        lax.all_gather(local_delta, "kv", axis=1, tiled=True),
    )
    key_all, value_all = (
        lax.all_gather(key_rows, "pb", axis=0, tiled=True),
        lax.all_gather(value_rows, "pb", axis=0, tiled=True),
    )
    query_sum, key_sum, value_sum = block_grads(
        query_all, grad_all, norm_all, delta_all, query_pos, key_all, value_all, key_pos
    )
    query_grad = lax.psum_scatter(query_sum, "kv", scatter_dimension=0, tiled=True)
    key_grad, value_grad = (
        lax.psum_scatter(key_sum, "pb", scatter_dimension=0, tiled=True),
        lax.psum_scatter(value_sum, "pb", scatter_dimension=0, tiled=True),
    )
    return (query_grad, key_grad, value_grad)


def solution(mesh):
    return jax.shard_map(
        shards,
        mesh=mesh,
        in_specs=(
            P(("pb", "kv"), None),
            P(("kv", "pb"), None),
            P(("kv", "pb"), None),
            P(("pb", "kv"), None),
            P(("pb", "kv"), None),
            P(None, ("pb", "kv")),
            P(),
        ),
        out_specs=(P(("pb", "kv"), None), P(("kv", "pb"), None), P(("kv", "pb"), None)),
        check_vma=False,
    )
```

profile of v0, /device:TPU:0, one launch (start us, length us, event | category | flops | bytes accessed | tf_op | source)
XLA Modules:
  0.0 233.3 jit_solution(10503284566190292486)
XLA Ops:
  7.2 0.0 all-gather.3.cloned.1.call-start
  7.2 0.7 all-gather.3.cloned.1.call-update
  7.9 0.0 all-gather.5.cloned.1.call-start
  8.0 0.7 all-gather.5.cloned.1.call-update
  8.7 0.0 reduce-scatter.6.cloned.1.call-start
  8.7 0.9 copy.25
  9.6 1.1 multiply_bitcast_fusion
  10.7 0.1 copy.41
  10.8 0.2 reduce_sum.9
  11.0 16.8 %all_gather.23 = f32[8,512]{0,1:T(8,128)S(1)} all-gather(f32[8,128]{0,1:T(8,128)S(1)} %bitcast.87), channel_id=1, replica_groups=mesh['pb'=8,'kv'=4] {'kv'}, dimensions={1}, use_global_device_ids=true | all-gather | bytes 20480 | tf_op jit(solution)/shard_map/all_gather | solution.py:78
  27.9 0.1 copy.26
  28.0 14.0 %all_gather.20 = f32[8,512]{1,0:T(8,128)S(1)} all-gather(f32[8,128]{1,0:T(8,128)} %param.14), channel_id=1, replica_groups=mesh['pb'=8,'kv'=4] {'kv'}, dimensions={1}, use_global_device_ids=true | all-gather | bytes 20480 | tf_op jit(solution)/shard_map/all_gather | solution.py:77
  42.0 9.4 %all_gather.19 = bf16[1024,128]{0,1:T(8,128)(2,1)S(1)} all-gather(bf16[128,128]{0,1:T(8,128)(2,1)S(1)} %copy.25), channel_id=1, replica_groups=mesh['pb'=8,'kv'=4] {'pb'}, dimensions={0}, use_global_device_ids=true | all-gather | bytes 294912 | tf_op jit(solution)/shard_map/all_gather | solution.py:81
  51.4 10.2 %all_gather.22 = bf16[1024,128]{1,0:T(8,128)(2,1)} all-gather(bf16[128,128]{1,0:T(8,128)(2,1)S(1)} %copy-done.3), channel_id=1, replica_groups=mesh['pb'=8,'kv'=4] {'pb'}, dimensions={0}, use_global_device_ids=true | all-gather | bytes 294912 | tf_op jit(solution)/shard_map/all_gather | solution.py:82
  61.6 0.1 dynamic-slice_bitcast_fusion.2
  61.7 1.5 copy.39
  63.2 7.9 %all-gather.5.cloned.1.call-done = bf16[512,1024]{1,0:T(8,128)(2,1)} async-done(((bf16[128,1024]{1,0:T(8,128)(2,1)}), bf16[512,1024]{1,0:T(8,128)(2,1)}) %all-gather.5.cloned.1.call-update) | async-done | bytes 1048592 | tf_op jit(solution)/shard_map/all_gather | solution.py:74
  71.1 2.5 %copy.40 = bf16[64,8,8,128]{3,2,1,0:T(8,128)(2,1)} copy(bf16[64,8,8,128]{3,1,2,0:T(8,128)(2,1)} %bitcast.86) | data formatting | bytes 2097152
  73.5 34.7 %while.15 = (s32[]{:T(128)}, f32[1024,128]{1,0:T(8,128)S(1)}, f32[1024,128]{1,0:T(8,128)S(1)}, f32[4,128,1024]{2,1,0:T(8,128)}, s32[1024]{0:T(1024)S(1)}, /*inde...) while((s32[]{:T(128)}, f32[1024,128]{1,0:T(8,128)S(1)}, ...), condition=%wide.region_2.3_spmd.clone, body=%wide.region_1.2_spmd.clone.sunk | while | flops 1354366976 | bytes 26904232 | solution.py:50
  73.6 0.1 broadcast_compare_fusion.2
  73.7 1.0 constant_dynamic-slice_fusion.4
  74.7 0.7 fusion.38
  75.4 1.4 fusion.41
  76.8 2.7 %multiply_convert_fusion.2 = bf16[128,8,1024]{2,0,1:T(8,128)(2,1)S(1)} fusion(f32[128,8,1024]{2,0,1:T(8,128)S(1)} %fusion.38, f32[128,8]{0,1:T(8,128)S(1)} %get-tuple-element.239, f32[128,8]{0,1:T(8,128)S(1)} %get-tuple-element.240, pred[128,1024]{1,0:T(8,128)(4,1)S(1)} %broadcast_compare_fusion.2, bf16[1024,128]{1,0:T(8,128)(2,1)} %get-tuple-element.280, ...), kind=kOutput, calls=%fused_computation.clone.1 | convolution fusion | flops 275775488 | bytes 6955008 | tf_op jit(solution)/shard_map/while/body/eval_jaxpr/tgd,cd->tgc/dot_general | solution.py:35
  79.5 0.8 fusion.40
  80.3 0.8 fusion.42
  81.2 0.2 copy.57
  81.4 0.8 constant_dynamic-update-slice_fusion.2
  82.2 0.1 broadcast_compare_fusion.2
  82.4 1.0 constant_dynamic-slice_fusion.4
  83.4 0.7 fusion.38
  84.1 1.4 fusion.41
  85.5 2.7 %multiply_convert_fusion.2 = bf16[128,8,1024]{2,0,1:T(8,128)(2,1)S(1)} fusion(f32[128,8,1024]{2,0,1:T(8,128)S(1)} %fusion.38, f32[128,8]{0,1:T(8,128)S(1)} %get-tuple-element.239, f32[128,8]{0,1:T(8,128)S(1)} %get-tuple-element.240, pred[128,1024]{1,0:T(8,128)(4,1)S(1)} %broadcast_compare_fusion.2, bf16[1024,128]{1,0:T(8,128)(2,1)} %get-tuple-element.280, ...), kind=kOutput, calls=%fused_computation.clone.1 | convolution fusion | flops 275775488 | bytes 6955008 | tf_op jit(solution)/shard_map/while/body/eval_jaxpr/tgd,cd->tgc/dot_general | solution.py:35
  88.2 0.8 fusion.40
  89.0 0.8 fusion.42
  89.9 0.2 copy.57
  90.1 0.8 constant_dynamic-update-slice_fusion.2
  90.9 0.1 broadcast_compare_fusion.2
  91.1 1.0 constant_dynamic-slice_fusion.4
  92.1 0.7 fusion.38
  92.8 1.4 fusion.41
  94.2 2.7 %multiply_convert_fusion.2 = bf16[128,8,1024]{2,0,1:T(8,128)(2,1)S(1)} fusion(f32[128,8,1024]{2,0,1:T(8,128)S(1)} %fusion.38, f32[128,8]{0,1:T(8,128)S(1)} %get-tuple-element.239, f32[128,8]{0,1:T(8,128)S(1)} %get-tuple-element.240, pred[128,1024]{1,0:T(8,128)(4,1)S(1)} %broadcast_compare_fusion.2, bf16[1024,128]{1,0:T(8,128)(2,1)} %get-tuple-element.280, ...), kind=kOutput, calls=%fused_computation.clone.1 | convolution fusion | flops 275775488 | bytes 6955008 | tf_op jit(solution)/shard_map/while/body/eval_jaxpr/tgd,cd->tgc/dot_general | solution.py:35
  96.9 0.8 fusion.40
  97.7 0.8 fusion.42
  98.5 0.2 copy.57
  98.7 0.9 constant_dynamic-update-slice_fusion.2
  99.6 0.1 broadcast_compare_fusion.2
  99.8 1.0 constant_dynamic-slice_fusion.4
  100.7 0.7 fusion.38
  101.4 1.4 fusion.41
  102.8 2.7 %multiply_convert_fusion.2 = bf16[128,8,1024]{2,0,1:T(8,128)(2,1)S(1)} fusion(f32[128,8,1024]{2,0,1:T(8,128)S(1)} %fusion.38, f32[128,8]{0,1:T(8,128)S(1)} %get-tuple-element.239, f32[128,8]{0,1:T(8,128)S(1)} %get-tuple-element.240, pred[128,1024]{1,0:T(8,128)(4,1)S(1)} %broadcast_compare_fusion.2, bf16[1024,128]{1,0:T(8,128)(2,1)} %get-tuple-element.280, ...), kind=kOutput, calls=%fused_computation.clone.1 | convolution fusion | flops 275775488 | bytes 6955008 | tf_op jit(solution)/shard_map/while/body/eval_jaxpr/tgd,cd->tgc/dot_general | solution.py:35
  105.5 0.8 fusion.40
  106.4 0.8 fusion.42
  107.2 0.2 copy.57
  107.4 0.8 constant_dynamic-update-slice_fusion.2
  108.3 0.8 copy-done
  109.1 0.0 reduce-scatter.8.cloned.1.call-start
  109.2 0.1 copy-done.1
  109.3 0.4 reduce-scatter.8.cloned.1.call-update
  109.7 0.0 reduce-scatter.4.cloned.1.call-start
  109.7 0.5 reduce-scatter.4.cloned.1.call-update
  110.3 32.5 %reduce-scatter.6.cloned.1.call-done = f32[128,128]{1,0:T(8,128)} async-done(((f32[1024,128]{1,0:T(8,128)}), f32[128,128]{1,0:T(8,128)}) %reduce-scatter.6.cloned.1.call-update) | async-done | bytes 65552 | tf_op jit(solution)/shard_map/reduce_scatter | solution.py:89
  142.8 37.6 %reduce-scatter.8.cloned.1.call-done = f32[128,128]{1,0:T(8,128)} async-done(((f32[1024,128]{1,0:T(8,128)}), f32[128,128]{1,0:T(8,128)}) %reduce-scatter.8.cloned.1.call-update) | async-done | bytes 65552 | tf_op jit(solution)/shard_map/reduce_scatter | solution.py:90
  180.4 46.4 %reduce-scatter.4.cloned.1.call-done = f32[128,1024]{1,0:T(8,128)} async-done(((f32[512,1024]{1,0:T(8,128)}), f32[128,1024]{1,0:T(8,128)}) %reduce-scatter.4.cloned.1.call-update) | async-done | bytes 524304 | tf_op jit(solution)/shard_map/reduce_scatter | solution.py:87
  (21 shorter events, 0.1 us)
Async XLA Ops:
  7.2 54.4 %copy-start.2 = (s32[4096]{0:T(1024)S(1)}, s32[4096]{0:T(1024)}, u32[]{:S(2)}) copy-start(s32[4096]{0:T(1024)} %param.15) | copy-start | bytes 49156
  7.2 44.2 %copy-start.3 = (bf16[128,128]{1,0:T(8,128)(2,1)S(1)}, bf16[128,128]{1,0:T(8,128)(2,1)}, u32[]{:S(2)}) copy-start(bf16[128,128]{1,0:T(8,128)(2,1)} %param.11) | copy-start | bytes 98308
  7.2 54.5 %all-gather.3.cloned.1.call-start = ((), (), s32[]{:S(2)}) async-start(), calls=%async_computation.3 | async-start | bytes 1310720 | tf_op jit(solution)/shard_map/all_gather | solution.py:73
  7.9 63.1 %all-gather.5.cloned.1.call-start = ((), (), s32[]{:S(2)}) async-start(), calls=%async_computation.4 | async-start | bytes 1310720 | tf_op jit(solution)/shard_map/all_gather | solution.py:74
  8.7 134.1 %reduce-scatter.6.cloned.1.call-start = ((), (), s32[]{:S(2)}) async-start(), calls=%async_computation.6 | async-start | bytes 589824 | tf_op jit(solution)/shard_map/reduce_scatter | solution.py:89
  28.0 45.6 %dynamic-slice-start = ((s32[4096]{0:T(1024)}, s32[]{:T(128)}), s32[1024]{0:T(1024)S(1)}, s32[]{:S(2)}) async-start(s32[4096]{0:T(1024)} %param.15, s32[]{:T(128)} %select_n.10), calls=%async_computation.8 | async-start | bytes 8704 | tf_op jit(solution)/shard_map/dynamic_slice | solution.py:70
  108.3 0.8 copy-start
  108.3 1.0 copy-start.1
  109.1 71.3 %reduce-scatter.8.cloned.1.call-start = ((), (), s32[]{:S(2)}) async-start(), calls=%async_computation.7 | async-start | bytes 589824 | tf_op jit(solution)/shard_map/reduce_scatter | solution.py:90
  109.7 117.1 %reduce-scatter.4.cloned.1.call-start = ((), (), s32[]{:S(2)}) async-start(), calls=%async_computation.5 | async-start | bytes 2621440 | tf_op jit(solution)/shard_map/reduce_scatter | solution.py:87
Sparse Core Ops, SparseCore 0:
  9.6 32.1 all-gather.2
  43.3 27.6 all-gather.4
  109.2 33.4 reduce-scatter.5
  146.3 34.0 reduce-scatter.7
  183.1 43.6 reduce-scatter.3
where the time goes:
time: 234 us; the launch traced here: 233 us
  waiting for transfers between devices  127 us (54%)
  blocking collectives  50.5 us (22%)
  matrix products  25.8 us (11%)
  local copies, waits for them, and re-layouts  14.2 us (6%)
  between operations  13.9 us (6%)
    reduce_scatter x1, waiting for transfers between devices, shards(): lax.psum_scatter(query_sum, 'kv', scatter_dimension=0, tiled=True)  46.4 us
    reduce_scatter x1, waiting for transfers between devices, shards(): lax.psum_scatter(value_sum, 'pb', scatter_dimension=0, tiled=True)  37.6 us
    reduce_scatter x1, waiting for transfers between devices, shards(): lax.psum_scatter(key_sum, 'pb', scatter_dimension=0, tiled=True)  32.5 us
    all_gather x1, blocking collectives, shards(): lax.all_gather(local_delta, 'kv', axis=1, tiled=True)  16.8 us
    all_gather x1, blocking collectives, shards(): lax.all_gather(log_norm, 'kv', axis=1, tiled=True)  14 us
    dot_general x4, matrix products, one_block(): jnp.einsum('tgd,cd->tgc', grad_block, value_part, preferred_element_type=...  10.8 us
    all_gather x1, blocking collectives, shards(): lax.all_gather(value_rows, 'pb', axis=0, tiled=True)  10.2 us
    all_gather x1, blocking collectives, shards(): lax.all_gather(key_rows, 'pb', axis=0, tiled=True)  9.37 us
  transfers between devices with their start and end apart: 5, of which 4 were waited for; matrix products, arithmetic and copies ran while one was open for 2% of the time, Pallas kernels for 0%

commit v1 on v0

v1 whole, which is shorter than its diff:
```python
import functools
import math

import jax
import jax.numpy as jnp
from jax import lax
from jax.experimental import pallas as pl
from jax.experimental.pallas import tpu as pltpu
from jax.sharding import PartitionSpec as P

MESH = pl.DeviceIdType.MESH
LOG2E = math.log2(math.e)
HIDDEN = -1e30


def flip(index, mask, count):
    total, bit = 0, 1
    while bit < count:
        digit = (index // bit) % 2
        total = total + bit * ((1 - digit) if mask & bit else digit)
        bit *= 2
    return total


def kernel(
    planes, layers, q_ref, k_ref, v_ref, o_ref, g_ref, n_ref, pos_ref,
    dq_ref, dk_ref, dv_ref,
    q_all, g_all, k_all, v_all, norm, delta, bias, dk_acc, dv_acc, dq_acc, dq_in,
    own, out1, in1, out2, in2,
    pair_send, pair_recv, z_send, z_recv, p_send, p_recv, r1_send, r1_recv, r2_send, r2_recv,
):
    pb, z = lax.axis_index("pb"), lax.axis_index("kv")
    p, core = pb // 2, pb % 2
    rows, heads = q_ref.shape[0], n_ref.shape[0]
    keys, width = k_ref.shape
    inv_root = 1.0 / math.sqrt(width)

    partner = {"pb": p * 2 + 1 - core, "kv": z}
    z_peers = [(z + step) % layers for step in range(layers)]
    p_peers = [flip(p, step, planes) for step in range(planes)]

    def above(step):
        return {"pb": pb, "kv": z_peers[step]}

    def beside(step):
        return {"pb": p_peers[step] * 2 + core, "kv": z}

    def remote(src, dst, send, recv, device):
        return pltpu.make_async_remote_copy(
            src_ref=src, dst_ref=dst, send_sem=send, recv_sem=recv,
            device_id=device, device_id_type=MESH,
        )

    peers = [partner] + [above(s) for s in range(1, layers)] + [beside(s) for s in range(1, planes)]
    barrier = pltpu.get_barrier_semaphore()
    for peer in peers:
        pl.semaphore_signal(barrier, inc=1, device_id=peer, device_id_type=MESH)
    pl.semaphore_wait(barrier, len(peers))

    def key_rows_of(layer):
        return pl.ds(pl.multiple_of(layer * keys, keys), keys)

    pending = []
    mine = key_rows_of(z)
    z_copies = {}
    for step in range(1, layers):
        pair = [
            remote(src, dst.at[p, mine], z_send.at[step - 1, i], z_recv.at[step - 1, i], above(step))
            for i, (src, dst) in enumerate(((k_ref, k_all), (v_ref, v_all)))
        ]
        for copy in pair:
            copy.start()
        z_copies[step] = pair
    p_copies = {}

    def spread(step_z):
        layer = (z + layers - step_z) % layers
        place = key_rows_of(layer)
        for step in range(1, planes):
            pair = []
            for i, (own, full) in enumerate(((k_ref, k_all), (v_ref, v_all))):
                src = own if step_z == 0 else full.at[p, place]
                copy = remote(
                    src, full.at[p, place], p_send.at[step - 1, step_z, i],
                    p_recv.at[step - 1, step_z, i], beside(step),
                )
                copy.start()
                pair.append(copy)
            p_copies[step, step_z] = pair

    spread(0)
    pair_copies = [
        remote(q_ref, q_all.at[pl.ds(rows, rows)], pair_send.at[0], pair_recv.at[0], partner),
        remote(g_ref, g_all.at[pl.ds(rows, rows)], pair_send.at[1], pair_recv.at[1], partner),
    ]
    for copy in pair_copies:
        copy.start()

    norm[:, :rows] = n_ref[...] * LOG2E
    for h in range(heads):
        part = slice(h * width, (h + 1) * width)
        product = g_ref[:, part].astype(jnp.float32) * o_ref[:, part].astype(jnp.float32)
        delta[h : h + 1, :rows] = jnp.sum(product.T, axis=0, keepdims=True)
    stat_copies = [
        remote(norm.at[:, pl.ds(0, rows)], norm.at[:, pl.ds(rows, rows)], pair_send.at[2], pair_recv.at[2], partner),
        remote(delta.at[:, pl.ds(0, rows)], delta.at[:, pl.ds(rows, rows)], pair_send.at[3], pair_recv.at[3], partner),
    ]
    for copy in stat_copies:
        copy.start()
    pair_copies += stat_copies
    q_all[:rows] = q_ref[...]
    g_all[:rows] = g_ref[...]
    k_all[p, mine] = k_ref[...]
    v_all[p, mine] = v_ref[...]

    pos_own = pos_ref[pl.ds(pb * layers + z, 1), :]
    pos_partner = pos_ref[pl.ds((p * 2 + 1 - core) * layers + z, 1), :]

    def make_bias(column):
        for layer in range(layers):
            block = layer * (2 * planes) + column * 2 + core
            row = pos_ref[pl.ds(block, 1), :]
            key_pos = jnp.broadcast_to(row, (rows, keys)).T
            place = slice(layer * keys, (layer + 1) * keys)
            bias[place, :rows] = jnp.where(key_pos <= pos_own, 0.0, HIDDEN)
            bias[place, rows:] = jnp.where(key_pos <= pos_partner, 0.0, HIDDEN)

    make_bias(p)
    for step in range(1, layers):
        for copy in z_copies[step]:
            copy.wait_recv()
        spread(step)
    for copy in pair_copies:
        copy.wait_recv()

    last = (((1,), (1,)), ((), ()))

    def compute(column, first):
        k_turned = k_all[column].T

        def one_head(h):
            part = pl.ds(pl.multiple_of(h * width, width), width)
            q, g = q_all[:, part], g_all[:, part]
            scores = lax.dot_general(k_all[column], q, last, preferred_element_type=jnp.float32)
            grad_probs = lax.dot_general(v_all[column], g, last, preferred_element_type=jnp.float32)
            probs = jnp.exp2(scores * (inv_root * LOG2E) - norm[pl.ds(h, 1), :] + bias[...])
            probs_low = probs.astype(jnp.bfloat16)
            grad_scores = (probs * (grad_probs - delta[pl.ds(h, 1), :])).astype(jnp.bfloat16)
            dv = jnp.dot(probs_low, g, preferred_element_type=jnp.float32)
            dk = jnp.dot(grad_scores, q, preferred_element_type=jnp.float32)
            dq = jnp.dot(k_turned, grad_scores, preferred_element_type=jnp.float32)
            return dv, dk, dq

        dk_acc[...] = jnp.zeros_like(dk_acc)
        dv_acc[...] = jnp.zeros_like(dv_acc)

        def body(i, carry):
            results = [one_head(2 * i), one_head(2 * i + 1)]
            dv_acc[...] += results[0][0] + results[1][0]
            dk_acc[...] += results[0][1] + results[1][1]
            for j in range(2):
                dq = results[j][2]
                for side in range(2):
                    half = dq[:, side * rows : (side + 1) * rows]
                    if first:
                        dq_acc[side, 2 * i + j] = half
                    else:
                        dq_acc[side, 2 * i + j] += half
            return carry

        lax.fori_loop(0, heads // 2, body, 0)

    compute(p, True)
    own[0] = dk_acc[...]
    own[1] = dv_acc[...]

    r1_copies = []
    for step in range(1, planes):
        make_bias(p_peers[step])
        for step_z in range(layers):
            for copy in p_copies[step, step_z]:
                copy.wait_recv()
        compute(p_peers[step], False)
        if step == planes - 1:
            back = remote(dq_acc.at[1], dq_in, pair_send.at[4], pair_recv.at[4], partner)
            back.start()
            pair_copies.append(back)
        out1[step - 1, 0] = dk_acc[...].astype(jnp.bfloat16)
        out1[step - 1, 1] = dv_acc[...].astype(jnp.bfloat16)
        copy = remote(
            out1.at[step - 1], in1.at[step - 1], r1_send.at[step - 1], r1_recv.at[step - 1], beside(step)
        )
        copy.start()
        r1_copies.append(copy)

    for copy in r1_copies:
        copy.wait_recv()
    r2_copies = []

    def layer_sum(layer):
        place = key_rows_of(layer)
        total = own[:, place]
        for step in range(1, planes):
            total = total + in1[step - 1, :, place].astype(jnp.float32)
        return total

    for step in range(1, layers):
        out2[step - 1] = layer_sum(z_peers[step]).astype(jnp.bfloat16)
        copy = remote(
            out2.at[step - 1], in2.at[step - 1], r2_send.at[step - 1], r2_recv.at[step - 1], above(step)
        )
        copy.start()
        r2_copies.append(copy)
    total = layer_sum(z)

    pair_copies[4].wait_recv()
    for h in range(heads):
        part = slice(h * width, (h + 1) * width)
        dq_ref[:, part] = ((dq_acc[0, h] + dq_in[h]) * inv_root).T

    for copy in r2_copies:
        copy.wait_recv()
    for step in range(1, layers):
        total = total + in2[step - 1].astype(jnp.float32)
    dk_ref[...] = total[0] * inv_root
    dv_ref[...] = total[1]

    sent = pair_copies + r1_copies + r2_copies
    for pair in list(z_copies.values()) + list(p_copies.values()):
        sent += pair
    for copy in sent:
        copy.wait_send()


def solution(mesh):
    planes, layers = mesh.shape["pb"] // 2, mesh.shape["kv"]

    def step(queries, key_rows, value_rows, output, out_grad, log_norm, positions):
        rows, columns = queries.shape
        keys, width = key_rows.shape
        heads = log_norm.shape[0]
        column = layers * keys
        low, full = jnp.bfloat16, jnp.float32
        vmem = pl.BlockSpec(memory_space=pltpu.VMEM)
        dma = pltpu.SemaphoreType.DMA
        return pl.pallas_call(
            functools.partial(kernel, planes, layers),
            out_shape=(
                jax.ShapeDtypeStruct((rows, columns), full),
                jax.ShapeDtypeStruct((keys, width), full),
                jax.ShapeDtypeStruct((keys, width), full),
            ),
            in_specs=[vmem] * 7,
            out_specs=(vmem, vmem, vmem),
            scratch_shapes=[
                pltpu.VMEM((2 * rows, columns), low),
                pltpu.VMEM((2 * rows, columns), low),
                pltpu.VMEM((planes, column, width), low),
                pltpu.VMEM((planes, column, width), low),
                pltpu.VMEM((heads, 2 * rows), full),
                pltpu.VMEM((heads, 2 * rows), full),
                pltpu.VMEM((column, 2 * rows), full),
                pltpu.VMEM((column, width), full),
                pltpu.VMEM((column, width), full),
                pltpu.VMEM((2, heads, width, rows), full),
                pltpu.VMEM((heads, width, rows), full),
                pltpu.VMEM((2, column, width), full),
                pltpu.VMEM((planes - 1, 2, column, width), low),
                pltpu.VMEM((planes - 1, 2, column, width), low),
                pltpu.VMEM((layers - 1, 2, keys, width), low),
                pltpu.VMEM((layers - 1, 2, keys, width), low),
                dma((5,)), dma((5,)),
                dma((layers - 1, 2)), dma((layers - 1, 2)),
                dma((planes - 1, layers, 2)), dma((planes - 1, layers, 2)),
                dma((planes - 1,)), dma((planes - 1,)),
                dma((layers - 1,)), dma((layers - 1,)),
            ],
            compiler_params=pltpu.CompilerParams(
                collective_id=0, has_side_effects=True, vmem_limit_bytes=60 * 2**20
            ),
        )(queries, key_rows, value_rows, output, out_grad, log_norm, positions.reshape(-1, rows))

    return jax.shard_map(
        step,
        mesh=mesh,
        in_specs=(
            P(("pb", "kv"), None),
            P(("kv", "pb"), None),
            P(("kv", "pb"), None),
            P(("pb", "kv"), None),
            P(("pb", "kv"), None),
            P(None, ("pb", "kv")),
            P(),
        ),
        out_specs=(P(("pb", "kv"), None), P(("kv", "pb"), None), P(("kv", "pb"), None)),
        check_vma=False,
    )
```

time: 234 us -> 48.8 us (0.21)
  waiting for transfers between devices: 127 us -> 0 us
  blocking collectives: 50.5 us -> 0 us
  Pallas kernels: 0 us -> 44.5 us
  matrix products: 25.8 us -> 0 us
  between operations: 13.9 us -> 0.65 us
  local copies, waits for them, and re-layouts: 14.2 us -> 3.41 us
    reduce_scatter x3 -> x0, waiting for transfers between devices: 116 us -> none  [the longest x1 46.4 us: shards(): lax.psum_scatter(query_sum, 'kv', scatter_dimension=0, tiled=True)]
    all_gather x4 -> x0, blocking collectives: 50.5 us -> none  [the longest x1 16.8 us: shards(): lax.all_gather(local_delta, 'kv', axis=1, tiled=True)]
    pallas_call x0 -> x1, Pallas kernels: none -> 44.5 us  [step(): pl.pallas_call(functools.partial(kernel, planes, layers), out_shape=(jax....]
    dot_general x20 -> x0, matrix products: 25.8 us -> none  [the longest x4 10.8 us: one_block(): jnp.einsum('tgd,cd->tgc', grad_block, value_part, preferred_element_type=...]
    all_gather x2 -> x0, waiting for transfers between devices: 7.89 us -> none  [the longest x1 7.89 us: shards(): lax.all_gather(out_grad, 'kv', axis=0, tiled=True)]
    dynamic_update_slice x8 -> x0, local copies, waits for them, and re-layouts: 4.18 us -> none  [block_grads(): lax.scan(one_block, (empty_grad, empty_grad), (query_blocks, grad_blocks,...]
    dynamic_slice x6 -> x0, local copies, waits for them, and re-layouts: 3.97 us -> none  [the longest x4 3.97 us: block_grads(): lax.scan(one_block, (empty_grad, empty_grad), (query_blocks, grad_blocks,...]
    unnamed x12 -> x7, local copies, waits for them, and re-layouts: 5.83 us -> 3.41 us
  transfers between devices with their start and end apart: 5 -> 0, of which waited for: 4 -> 0; matrix products, arithmetic and copies ran while one was open for 2% -> 0% of each run, Pallas kernels for 0% -> 0%
where the time goes in v1:
time: 48.8 us; the launch traced here: 48.6 us
  Pallas kernels  44.5 us (91%)
  local copies, waits for them, and re-layouts  3.41 us (7%)
  between operations  0.65 us (1%)
    pallas_call x1, Pallas kernels, step(): pl.pallas_call(functools.partial(kernel, planes, layers), out_shape=(jax....  44.5 us
    unnamed x7, local copies, waits for them, and re-layouts  3.41 us

profile of v1, /device:TPU:0, one launch (start us, length us, event | category | flops | bytes accessed | tf_op | source)
XLA Modules:
  0.0 48.6 jit_solution(1510687288830866414)
XLA Ops:
  0.6 44.5 %shard_map.94 = (f32[128,1024]{1,0:T(8,128)}, f32[128,128]{1,0:T(8,128)}, f32[128,128]{1,0:T(8,128)}) custom-call(bf16[128,1024]{1,0:T(8,128)(2,1)} %q_ref.1, bf16[128,128]{1,0:T(8,128)(2,1)} %k_ref.1, bf16[128,128]{1,0:T(8,128)(2,1)} %v_ref.1, bf16[128,1024]{1,0:T(8,128)(2,1)} %o_ref.1, bf16[128,1024]{1,0:T(8,128)(2,1)} %g_ref.1, f32[8,128]{1,0:T(8,128)} %n_ref.1, ...), custom_call_target="tpu_custom_call" | custom-call | tf_op jit(solution)/shard_map/pallas_call | solution.py:246
  45.2 0.0 copy-start.1
  45.2 1.9 %copy.13 = f32[128,1024]{1,0:T(8,128)} copy(f32[128,1024]{1,0:T(8,128)} %get-tuple-element.6) | data formatting | bytes 1048576
  47.1 0.0 copy-done.1
  47.1 0.0 copy-start
  47.1 0.6 %copy.14 = f32[128,128]{1,0:T(8,128)} copy(f32[128,128]{1,0:T(8,128)S(1)} %copy-done.1) | data formatting | bytes 131072
  47.7 0.2 copy-done
  48.0 0.6 %copy.15 = f32[128,128]{1,0:T(8,128)} copy(f32[128,128]{1,0:T(8,128)S(1)} %copy-done) | data formatting | bytes 131072
Async XLA Ops:
  45.2 1.9 %copy-start.1 = (f32[128,128]{1,0:T(8,128)S(1)}, f32[128,128]{1,0:T(8,128)}, u32[]{:S(2)}) copy-start(f32[128,128]{1,0:T(8,128)} %get-tuple-element.7) | copy-start | bytes 196612
  47.1 0.9 %copy-start = (f32[128,128]{1,0:T(8,128)S(1)}, f32[128,128]{1,0:T(8,128)}, u32[]{:S(2)}) copy-start(f32[128,128]{1,0:T(8,128)} %get-tuple-element.8) | copy-start | bytes 196612
